TPU v7x, 512 devices: a whole 4x4x16 slice. The times are simulated.
512 devices in a mesh: dp: 2 (over z_hi), fsdp: 16 (over z_lo, core), tile: 16 (over y, x).
Axes of the slice: x: 4, y: 4, z: 16 (z_hi: 2, z_lo: 8; z = z_hi * 8 + z_lo), core: 2. Of those that a mesh axis runs over, the one named last changes fastest.
Arguments:
- tokens: bfloat16 [32, 8, 512, 1536], P(('dp', 'fsdp'), None, 'tile'), may hold values from -6 to 6
- norm_gain: float32 [1536], replicated, may hold values from 0.25 to 1.75
- query_key_value_weight: bfloat16 [1536, 2304], P('fsdp'), may hold values from -5 to 5
- out_weight: bfloat16 [768, 1536], P('fsdp'), may hold values from -0.21875 to 0.21875
- head_weight: bfloat16 [1536, 320], P('fsdp'), may hold values from -0.15625 to 0.15625
- coarse: float32 [32, 20, 8, 512], P(('dp', 'fsdp'), None, None, 'tile'), may hold values from -36 to 36
- grad_fine: float32 [32, 20, 32, 2048], P(('dp', 'fsdp'), None, None, 'tile'), may hold values from -0.6 to 0.6
Outputs:
- fine_grid: float32 [32, 20, 32, 2048], P(('dp', 'fsdp'), None, None, 'tile')
- grad_tokens: bfloat16 [32, 8, 512, 1536], P(('dp', 'fsdp'), None, 'tile')
- grad_head: float32 [1536, 320], P('fsdp')
All inputs are finite; a program needn't handle non-finite values.
Results may differ from a plain program's by a relative error of at most 0.0059.
Values may be sent and summed in bfloat16 or wider, within the bound.
No kernel may reach another device: no remote copies, remote signals or barrier semaphores. Data moves between devices by JAX's collectives and lax.ppermute only.
A program may use at most 64 MiB of HBM per device.

v0:
```python
import jax
import jax.numpy as jnp
from jax import lax
from jax.sharding import PartitionSpec as P

D = 1536
HEADS = 8
HEAD_DIM = 96
VARS = 20
MARGIN = 8
INNER = 768
HEAD_OUT = 320
EPSILON = 1e-05


def with_halo(shard, sides, width):
    for axis, dim in sides:
        devices, length = (lax.axis_size(axis), shard.shape[dim])
        up = [(i, (i + 1) % devices) for i in range(devices)]
        down = [(j, i) for i, j in up]
        last = lax.slice_in_dim(shard, length - width, length, axis=dim)
        leading = lax.slice_in_dim(shard, 0, width, axis=dim)
        before = lax.ppermute(last, axis, up)
        after = lax.ppermute(leading, axis, down)
        shard = jnp.concatenate([before, shard, after], axis=dim)
    return shard


def from_behind(value, axis, steps):
    count = lax.axis_size(axis)
    pairs = [(source, (source + steps) % count) for source in range(count)]
    return lax.ppermute(value, axis, pairs)


def layer_norm(values):
    average = jnp.mean(values, axis=-1, keepdims=True)
    centred = values - average
    variance = jnp.mean(centred * centred, axis=-1, keepdims=True)
    inverse_dev = lax.rsqrt(variance + EPSILON)
    return (centred * inverse_dev, inverse_dev)


def norm_backward(grad_normed, standard, inverse_dev, norm_gain):
    grad_standard = grad_normed * norm_gain
    first_mean = jnp.mean(grad_standard, axis=-1, keepdims=True)
    second_mean = jnp.mean(grad_standard * standard, axis=-1, keepdims=True)
    return inverse_dev * (grad_standard - first_mean - standard * second_mean)


def attend_forward(queries, keys_values):
    query_count = queries.shape[0]
    key_count = keys_values.shape[0]
    score_scale = HEAD_DIM ** (-0.5)
    query_heads = queries.reshape(query_count, HEADS, HEAD_DIM)
    key_heads = keys_values[:, :INNER].reshape(key_count, HEADS, HEAD_DIM)
    value_heads = keys_values[:, INNER:].reshape(key_count, HEADS, HEAD_DIM)
    scores = (
        jnp.einsum("qhd,khd->hqk", query_heads, key_heads, preferred_element_type=jnp.float32)
        * score_scale
    )
    biggest = jnp.max(scores, axis=-1, keepdims=True)
    exponent = jnp.exp(scores - biggest)
    softmax_out = exponent / jnp.sum(exponent, axis=-1, keepdims=True)
    softmax_low = softmax_out.astype(jnp.bfloat16)
    attended = jnp.einsum(
        "hqk,khd->qhd", softmax_low, value_heads, preferred_element_type=jnp.float32
    )
    return (attended.astype(jnp.bfloat16).reshape(query_count, INNER), softmax_out)


def attend_backward(softmax_out, queries, keys_values, grad_attended):
    query_count = queries.shape[0]
    key_count = keys_values.shape[0]
    score_scale = HEAD_DIM ** (-0.5)
    query_heads = queries.reshape(query_count, HEADS, HEAD_DIM)
    key_heads = keys_values[:, :INNER].reshape(key_count, HEADS, HEAD_DIM)
    value_heads = keys_values[:, INNER:].reshape(key_count, HEADS, HEAD_DIM)
    grad_heads = grad_attended.reshape(query_count, HEADS, HEAD_DIM)
    softmax_low = softmax_out.astype(jnp.bfloat16)
    grad_values = jnp.einsum(
        "hqk,qhd->khd", softmax_low, grad_heads, preferred_element_type=jnp.float32
    )
    grad_weights = jnp.einsum(
        "qhd,khd->hqk", grad_heads, value_heads, preferred_element_type=jnp.float32
    )
    weighted = jnp.sum(softmax_out * grad_weights, axis=-1, keepdims=True)
    grad_scores = (softmax_out * (grad_weights - weighted)).astype(jnp.bfloat16)
    grad_queries = (
        jnp.einsum("hqk,khd->qhd", grad_scores, key_heads, preferred_element_type=jnp.float32)
        * score_scale
    )
    grad_keys = (
        jnp.einsum("hqk,qhd->khd", grad_scores, query_heads, preferred_element_type=jnp.float32)
        * score_scale
    )
    pair_gradient_rows = jnp.concatenate(
        [grad_keys.reshape(key_count, INNER), grad_values.reshape(key_count, INNER)], axis=1
    )
    return (grad_queries.astype(jnp.bfloat16).reshape(query_count, INNER), pair_gradient_rows)


def interp_weights(fine_index):
    coarse_cell = fine_index // 4
    phase_index = fine_index % 4
    lower_shift = (phase_index < 2).astype(jnp.int32)
    upper_weight = (2 * phase_index - 3 + 8 * lower_shift).astype(jnp.float32) / 8.0
    return (coarse_cell - lower_shift, upper_weight)


def build_matrix(lower_cell, upper_cell, upper_weight, count):
    columns = jnp.arange(count, dtype=jnp.int32)
    lower_part = jnp.where(
        columns[None, :] == lower_cell[:, None], 1.0 - upper_weight[:, None], 0.0
    )
    upper_portion = jnp.where(columns[None, :] == upper_cell[:, None], upper_weight[:, None], 0.0)
    return lower_part + upper_portion


def contract_last(left_side, right_side):
    return lax.dot_general(
        left_side, right_side, (((1,), (1,)), ((), ())), preferred_element_type=jnp.float32
    )


def shards(tokens, norm_gain, query_key_value_weight, out_weight, head_weight, coarse, grad_fine):
    lat_rows = tokens.shape[1]
    lon_cols = tokens.shape[2]
    row_count = lat_rows * lon_cols
    flattened_rows = tokens[0].reshape(row_count, D).astype(jnp.float32)
    standard, inverse_dev = layer_norm(flattened_rows)
    normed = (standard * norm_gain).astype(jnp.bfloat16)
    full_qkv = lax.all_gather(query_key_value_weight, "fsdp", axis=0, tiled=True)
    projected = jnp.dot(normed, full_qkv, preferred_element_type=jnp.float32).astype(jnp.bfloat16)
    queries = projected[:, :INNER]
    pairs_local = projected[:, INNER:]
    margin_pairs = with_halo(
        pairs_local.reshape(lat_rows, lon_cols, 2 * INNER), (("tile", 1),), MARGIN
    )
    keys_values = margin_pairs.reshape(lat_rows * (lon_cols + 2 * MARGIN), 2 * INNER)
    attended, softmax_out = attend_forward(queries, keys_values)
    full_out = lax.all_gather(out_weight, "fsdp", axis=0, tiled=True)
    mixed_out = jnp.dot(attended, full_out, preferred_element_type=jnp.float32)
    hidden = (flattened_rows + mixed_out).astype(jnp.bfloat16)
    full_head = lax.all_gather(head_weight, "fsdp", axis=0, tiled=True)
    head_out = jnp.dot(hidden, full_head, preferred_element_type=jnp.float32)
    fine_head = (
        head_out.reshape(lat_rows, lon_cols, VARS, 4, 4)
        .transpose(2, 0, 3, 1, 4)
        .reshape(VARS, 4 * lat_rows, 4 * lon_cols)
    )
    coarse_padded_grid = with_halo(coarse[0], (("tile", 2),), 1)
    lat_lower, lat_upper_weight = interp_weights(jnp.arange(4 * lat_rows, dtype=jnp.int32))
    latitude_matrix = build_matrix(
        jnp.clip(lat_lower, 0, lat_rows - 1),
        jnp.clip(lat_lower + 1, 0, lat_rows - 1),
        lat_upper_weight,
        lat_rows,
    )
    lon_lower, lon_upper_weight = interp_weights(jnp.arange(4 * lon_cols, dtype=jnp.int32))
    lon_matrix = build_matrix(lon_lower + 1, lon_lower + 2, lon_upper_weight, lon_cols + 2)
    incomplete_grid = jnp.einsum(
        "lj,kji->kli", latitude_matrix, coarse_padded_grid, precision=lax.Precision.HIGHEST
    )
    residual = jnp.einsum(
        "vrb,cb->vrc", incomplete_grid, lon_matrix, precision=lax.Precision.HIGHEST
    )
    fine_grid = fine_head + residual
    grad_rows = (
        grad_fine[0]
        .reshape(VARS, lat_rows, 4, lon_cols, 4)
        .transpose(1, 3, 0, 2, 4)
        .reshape(row_count, HEAD_OUT)
    )
    grad_rows = grad_rows.astype(jnp.bfloat16)
    head_term = lax.dot_general(
        hidden, grad_rows, (((0,), (0,)), ((), ())), preferred_element_type=jnp.float32
    )
    head_block = lax.psum_scatter(head_term, "fsdp", scatter_dimension=0, tiled=True)
    grad_head = lax.psum(head_block, ("dp", "tile"))
    grad_hidden = contract_last(grad_rows, full_head)
    grad_attended = contract_last(grad_hidden.astype(jnp.bfloat16), full_out).astype(jnp.bfloat16)
    grad_queries, pair_gradient_rows = attend_backward(
        softmax_out, queries, keys_values, grad_attended
    )
    pair_gradient_rows = pair_gradient_rows.reshape(lat_rows, lon_cols + 2 * MARGIN, 2 * INNER)
    from_left = from_behind(pair_gradient_rows[:, lon_cols + MARGIN :], "tile", 1)
    from_right = from_behind(pair_gradient_rows[:, :MARGIN], "tile", -1)
    own_cells = pair_gradient_rows[:, MARGIN : MARGIN + lon_cols]
    own_cells = own_cells + jnp.pad(from_left, ((0, 0), (0, lon_cols - MARGIN), (0, 0)))
    own_cells = own_cells + jnp.pad(from_right, ((0, 0), (lon_cols - MARGIN, 0), (0, 0)))
    grad_all = jnp.concatenate(
        [grad_queries, own_cells.reshape(row_count, 2 * INNER).astype(jnp.bfloat16)], axis=1
    )
    grad_normed = contract_last(grad_all, full_qkv)
    grad_input = grad_hidden + norm_backward(grad_normed, standard, inverse_dev, norm_gain)
    grad_tokens = grad_input.astype(jnp.bfloat16).reshape(1, lat_rows, lon_cols, D)
    return (fine_grid[None], grad_tokens, grad_head)


def solution(mesh):
    placed = (
        P(("dp", "fsdp"), None, "tile", None),
        P(),
        P("fsdp", None),
        P("fsdp", None),
        P("fsdp", None),
        P(("dp", "fsdp"), None, None, "tile"),
        P(("dp", "fsdp"), None, None, "tile"),
    )
    return jax.shard_map(
        shards,
        mesh=mesh,
        in_specs=placed,
        out_specs=(
            P(("dp", "fsdp"), None, None, "tile"),
            P(("dp", "fsdp"), None, "tile", None),
            P("fsdp", None),
        ),
        check_vma=False,
    )
```

profile of v0, /device:TPU:2, one launch (start us, length us, event | category | flops | bytes accessed | tf_op | source)
XLA Modules:
  0.0 943.6 jit_solution(4857148850893295786)
XLA Ops:
  10.4 3.4 collective-permute-start.2
  13.8 6.3 collective-permute-start.3
  25.7 46.6 %all_gather.11 = bf16[1536,320]{1,0:T(8,128)(2,1)S(1)} all-gather(bf16[96,320]{1,0:T(8,128)(2,1)} %param.11), channel_id=1, replica_groups=mesh['dp'=2,'fsdp'=16,'tile'=16] {'fsdp'}, dimensions={0}, use_global_device_ids=true | all-gather | bytes 1044480 | tf_op jit(solution)/shard_map/all_gather | solution.py:144
  75.7 2.1 convolution_bitcast_fusion.1
  77.8 55.1 %all-gather.3.cloned.1.call-done = bf16[1536,2304]{1,0:T(8,128)(2,1)} async-done(((bf16[96,2304]{1,0:T(8,128)(2,1)}), bf16[1536,2304]{1,0:T(8,128)(2,1)}) %all-gather.3.cloned.1.call-update) | async-done | bytes 7077904 | tf_op jit(solution)/shard_map/all_gather | solution.py:132
  132.9 5.3 convolution_convert_fusion
  140.0 3.2 collective-permute-start
  143.2 2.8 collective-permute-start.1
  146.0 86.6 %all-gather.5.cloned.1.call-done = bf16[768,1536]{1,0:T(8,128)(2,1)} async-done(((bf16[48,1536]{1,0:T(8,128)(2,1)}), bf16[768,1536]{1,0:T(8,128)(2,1)}) %all-gather.5.cloned.1.call-update) | async-done | bytes 2359312 | tf_op jit(solution)/shard_map/all_gather | solution.py:141
  232.6 3.2 convolution_convert_fusion.1
  235.8 1.9 copy.24
  237.8 1.8 slice.50
  239.6 1.9 copy.18
  243.9 2.1 copy.29
  246.1 2.1 copy.28
  248.2 4.0 fusion.57
  252.2 2.9 convolution_convert_fusion.2
  257.3 2.0 fusion.60
  260.7 3.0 copy.20
  263.8 3.0 copy.21
  266.8 2.6 convolution_bitcast_fusion
  271.0 2.7 concatenate.20
  274.9 3.0 multiply_reduce_fusion
  281.9 1.9 concatenate.19
  287.6 3.4 collective-permute-start.4
  291.1 2.8 collective-permute-start.5
  296.7 3.5 collective-permute-done.4
  300.2 3.3 collective-permute-done.5
  305.2 6.3 fusion.52
  311.6 73.0 %reduce-scatter.2.cloned.1.call-done = f32[96,320]{1,0:T(8,128)} async-done(((f32[1536,320]{1,0:T(8,128)}), f32[96,320]{1,0:T(8,128)}) %reduce-scatter.2.cloned.1.call-update) | async-done | bytes 122896 | tf_op jit(solution)/shard_map/reduce_scatter | solution.py:178
  384.5 2.9 add_convert_fusion
  387.4 548.1 %all-reduce.4.cloned.1.call-done = f32[96,320]{1,0:T(8,128)} async-done(((f32[96,320]{1,0:T(8,128)}), f32[96,320]{1,0:T(8,128)}) %all-reduce.4.cloned.1.call-update) | async-done | bytes 122896 | tf_op jit(solution)/shard_map/psum | solution.py:179
  (101 shorter events, 36.6 us)
Async XLA Ops:
  7.2 14.4 %copy-start = (bf16[1,8,32,1536]{3,2,1,0:T(8,128)(2,1)S(1)}, bf16[1,8,32,1536]{3,2,1,0:T(8,128)(2,1)}, u32[]{:S(2)}) copy-start(bf16[1,8,32,1536]{3,2,1,0:T(8,128)(2,1)} %param.7) | copy-start | bytes 2359300
  7.2 14.8 %copy-start.19 = (f32[1,20,32,128]{3,2,1,0:T(8,128)S(1)}, f32[1,20,32,128]{3,2,1,0:T(8,128)}, u32[]{:S(2)}) copy-start(f32[1,20,32,128]{3,2,1,0:T(8,128)} %param.13) | copy-start | bytes 983044
  7.2 125.7 %all-gather.3.cloned.1.call-start = ((), (), s32[]{:S(2)}) async-start(), calls=%async_computation.1 | async-start | bytes 7520256 | tf_op jit(solution)/shard_map/all_gather | solution.py:132
  7.9 224.7 %all-gather.5.cloned.1.call-start = ((), (), s32[]{:S(2)}) async-start(), calls=%async_computation.2 | async-start | bytes 2506752 | tf_op jit(solution)/shard_map/all_gather | solution.py:141
  8.7 375.8 %reduce-scatter.2.cloned.1.call-start = ((), (), s32[]{:S(2)}) async-start(), calls=%async_computation.3 | async-start | bytes 2506752 | tf_op jit(solution)/shard_map/reduce_scatter | solution.py:178
  10.4 65.2 %collective-permute-start.2 = (f32[20,8,1]{2,1,0:T(8,128)}, f32[20,8,1]{2,1,0:T(8,128)}, u32[]{:S(2)}, u32[]{:S(2)}) collective-permute-start(f32[20,8,1]{2,1,0:T(8,128)} %get-tuple-element.11), channel_id=1, source_target_pairs={{0,1},{1,2},{2,3},{3,4},{4,5},{5,6},{6,7},{7,8},{8,9},{9,10},{10,1... | collective-permute-start | bytes 1928 | tf_op jit(solution)/shard_map/ppermute | solution.py:23
  13.8 61.8 %collective-permute-start.3 = (f32[20,8,1]{2,1,0:T(8,128)}, f32[20,8,1]{2,1,0:T(8,128)}, u32[]{:S(2)}, u32[]{:S(2)}) collective-permute-start(f32[20,8,1]{2,1,0:T(8,128)} %get-tuple-element.12), channel_id=1, source_target_pairs={{1,0},{2,1},{3,2},{4,3},{5,4},{6,5},{7,6},{8,7},{9,8},{10,9},{11,1... | collective-permute-start | bytes 1928 | tf_op jit(solution)/shard_map/ppermute | solution.py:24
  72.3 1.6 copy-start.20
  72.3 3.4 copy-start.15
  138.2 1.8 copy-start.14
  140.0 101.5 %collective-permute-start = (bf16[8,8,1536]{2,1,0:T(8,128)(2,1)}, bf16[8,8,1536]{2,1,0:T(8,128)(2,1)}, u32[]{:S(2)}, u32[]{:S(2)}) collective-permute-start(bf16[8,8,1536]{2,1,0:T(8,128)(2,1)} %get-tuple-element.9), channel_id=1, source_target_pairs={{0,1},{1,2},{2,3},{3,4},{4,5},{5,6},{6,7},{7,8},{8,9},{9,10},{10,1... | collective-permute-start | bytes 589832 | tf_op jit(solution)/shard_map/ppermute | solution.py:23
  143.2 98.3 %collective-permute-start.1 = (bf16[8,8,1536]{2,1,0:T(8,128)(2,1)}, bf16[8,8,1536]{2,1,0:T(8,128)(2,1)}, u32[]{:S(2)}, u32[]{:S(2)}) collective-permute-start(bf16[8,8,1536]{2,1,0:T(8,128)(2,1)} %get-tuple-element.10), channel_id=1, source_target_pairs={{1,0},{2,1},{3,2},{4,3},{5,4},{6,5},{7,6},{8,7},{9,8},{10,9},{11,1... | collective-permute-start | bytes 589832 | tf_op jit(solution)/shard_map/ppermute | solution.py:24
  252.2 2.9 copy-start.4
  256.0 1.3 copy-start.10
  257.3 2.0 copy-start.12
  273.7 661.8 %all-reduce.4.cloned.1.call-start = ((), (), s32[]{:S(2)}) async-start(), calls=%async_computation.4 | async-start | bytes 294912 | tf_op jit(solution)/shard_map/psum | solution.py:179
  274.9 3.0 copy-start.3
  277.9 1.9 copy-start.9
  283.8 1.3 copy-start.8
  285.0 8.9 copy-start.2
  285.0 8.9 copy-start.6
  285.2 1.5 copy-start.5
  287.6 12.6 %collective-permute-start.4 = (f32[8,8,1536]{2,1,0:T(8,128)}, f32[8,8,1536]{2,1,0:T(8,128)}, u32[]{:S(2)}, u32[]{:S(2)}) collective-permute-start(f32[8,8,1536]{2,1,0:T(8,128)} %get-tuple-element.5), channel_id=1, source_target_pairs={{0,1},{1,2},{2,3},{3,4},{4,5},{5,6},{6,7},{7,8},{8,9},{9,10},{10,1... | collective-permute-start | bytes 1179656 | tf_op jit(solution)/shard_map/ppermute | solution.py:32
  291.0 4.5 copy-start.11
  291.0 4.5 copy-start.13
  291.0 4.5 copy-start.22
  291.0 4.5 copy-start.23
  291.0 4.5 copy-start.24
  291.1 4.5 copy-start.25
  291.1 12.4 %collective-permute-start.5 = (f32[8,8,1536]{2,1,0:T(8,128)}, f32[8,8,1536]{2,1,0:T(8,128)}, u32[]{:S(2)}, u32[]{:S(2)}) collective-permute-start(f32[8,8,1536]{2,1,0:T(8,128)} %get-tuple-element.6), channel_id=1, source_target_pairs={{0,15},{1,0},{2,1},{3,2},{4,3},{5,4},{6,5},{7,6},{8,7},{9,8},{10,9... | collective-permute-start | bytes 1179656 | tf_op jit(solution)/shard_map/ppermute | solution.py:32
  296.7 8.5 copy-start.18
  296.7 8.6 copy-start.21
  (4 other events, 4.4 us)
Sparse Core Ops, SparseCore 0:
  10.1 122.7 all-gather.2
  135.0 97.5 all-gather.4
  273.8 110.6 reduce-scatter.1
  387.3 548.2 all-reduce.3
where the time goes:
time: 945 us; the launch traced here: 944 us
  waiting for transfers between devices  771 us (82%)
  blocking collectives  46.6 us (5%)
  local copies, waits for them, and re-layouts  41.8 us (4%)
  matrix products  37.3 us (4%)
  starting transfers between devices  22.1 us (2%)
  between operations  14.2 us (2%)
  other arithmetic  10.8 us (1%)
    psum x1, waiting for transfers between devices, shards(): grad_head = lax.psum(head_block, ('dp', 'tile'))  548 us
    all_gather x1, waiting for transfers between devices, shards(): full_out = lax.all_gather(out_weight, 'fsdp', axis=0, tiled=True)  86.6 us
    reduce_scatter x1, waiting for transfers between devices, shards(): lax.psum_scatter(head_term, 'fsdp', scatter_dimension=0, tiled=True)  73 us
    all_gather x1, waiting for transfers between devices, shards(): lax.all_gather(query_key_value_weight, 'fsdp', axis=0, tiled=True)  55.1 us
    all_gather x1, blocking collectives, shards(): full_head = lax.all_gather(head_weight, 'fsdp', axis=0, tiled=True)  46.6 us
  transfers between devices with their start and end apart: 10, of which 6 were waited for; matrix products, arithmetic and copies ran while one was open for 5% of the time, Pallas kernels for 0%

commit v1 on v0

--- a/solution.py
+++ b/solution.py
@@ -176,7 +176,7 @@
         hidden, grad_rows, (((0,), (0,)), ((), ())), preferred_element_type=jnp.float32
     )
     head_block = lax.psum_scatter(head_term, "fsdp", scatter_dimension=0, tiled=True)
-    grad_head = lax.psum(head_block, ("dp", "tile"))
+    grad_head = jnp.sum(lax.all_gather(head_block, ("dp", "tile")), axis=0)
     grad_hidden = contract_last(grad_rows, full_head)
     grad_attended = contract_last(grad_hidden.astype(jnp.bfloat16), full_out).astype(jnp.bfloat16)
     grad_queries, pair_gradient_rows = attend_backward(

time: 945 us -> 537 us (0.57)
  the two profiles are of different devices: /device:TPU:2 before, /device:TPU:96 now
where the time goes in v1:
time: 537 us; the launch traced here: 536 us
  waiting for transfers between devices  367 us (68%)
  blocking collectives  49.9 us (9%)
  matrix products  35.7 us (7%)
  local copies, waits for them, and re-layouts  31.5 us (6%)
  starting transfers between devices  26 us (5%)
  between operations  14.3 us (3%)
  other arithmetic  11.4 us (2%)
    reduce_scatter x1, waiting for transfers between devices, shards(): lax.psum_scatter(head_term, 'fsdp', scatter_dimension=0, tiled=True)  110 us
    all_gather x1, waiting for transfers between devices, shards(): lax.all_gather(query_key_value_weight, 'fsdp', axis=0, tiled=True)  92.6 us
    all_gather x1, waiting for transfers between devices, shards(): grad_head = jnp.sum(lax.all_gather(head_block, ('dp', 'tile')), axis=0)  78.6 us
    all_gather x1, waiting for transfers between devices, shards(): full_out = lax.all_gather(out_weight, 'fsdp', axis=0, tiled=True)  66.7 us
    all_gather x1, blocking collectives, shards(): full_head = lax.all_gather(head_weight, 'fsdp', axis=0, tiled=True)  49.9 us
    ppermute x2, starting transfers between devices, with_halo(): after = lax.ppermute(leading, axis, down)  13 us
    ppermute x2, waiting for transfers between devices, from_behind(): return lax.ppermute(value, axis, pairs)  11.9 us
  transfers between devices with their start and end apart: 10, of which 7 were waited for; matrix products, arithmetic and copies ran while one was open for 12% of the time, Pallas kernels for 0%

profile of v1, /device:TPU:96, one launch (start us, length us, event | category | flops | bytes accessed | tf_op | source)
XLA Modules:
  0.0 535.7 jit_solution(3986231864766762101)
XLA Ops:
  10.9 92.6 %all-gather.5.cloned.1.call-done = bf16[1536,2304]{1,0:T(8,128)(2,1)} async-done(((bf16[96,2304]{1,0:T(8,128)(2,1)}), bf16[1536,2304]{1,0:T(8,128)(2,1)}) %all-gather.5.cloned.1.call-update) | async-done | bytes 7077904 | tf_op jit(solution)/shard_map/all_gather | solution.py:132
  103.5 5.0 convolution_convert_fusion
  109.4 6.7 %collective-permute-start.1 = (bf16[8,8,1536]{2,1,0:T(8,128)(2,1)}, bf16[8,8,1536]{2,1,0:T(8,128)(2,1)}, u32[]{:S(2)}, u32[]{:S(2)}) collective-permute-start(bf16[8,8,1536]{2,1,0:T(8,128)(2,1)} %get-tuple-element.10), channel_id=1, source_target_pairs={{1,0},{2,1},{3,2},{4,3},{5,4},{6,5},{7,6},{8,7},{9,8},{10,9},{11,1... | collective-permute-start | bytes 589832 | tf_op jit(solution)/shard_map/ppermute | solution.py:24
  116.1 1.9 collective-permute-start
  121.2 6.0 %collective-permute-done = bf16[8,8,1536]{2,1,0:T(8,128)(2,1)} collective-permute-done((bf16[8,8,1536]{2,1,0:T(8,128)(2,1)}, bf16[8,8,1536]{2,1,0:T(8,128)(2,1)}, u32[]{:S(2)}, u32[]{:S(2)}) %collective-permute-start) | collective-permute-done | bytes 196640 | tf_op jit(solution)/shard_map/ppermute | solution.py:23
  129.1 2.8 fusion.57
  131.9 2.6 convolution_convert_fusion.2
  134.5 66.7 %all-gather.7.cloned.1.call-done = bf16[768,1536]{1,0:T(8,128)(2,1)} async-done(((bf16[48,1536]{1,0:T(8,128)(2,1)}), bf16[768,1536]{1,0:T(8,128)(2,1)}) %all-gather.7.cloned.1.call-update) | async-done | bytes 2359312 | tf_op jit(solution)/shard_map/all_gather | solution.py:141
  201.2 2.5 fusion.4
  204.6 2.1 fusion.60
  206.7 109.7 %reduce-scatter.2.cloned.1.call-done = f32[96,320]{1,0:T(8,128)} async-done(((f32[1536,320]{1,0:T(8,128)}), f32[96,320]{1,0:T(8,128)}) %reduce-scatter.2.cloned.1.call-update) | async-done | bytes 122896 | tf_op jit(solution)/shard_map/reduce_scatter | solution.py:178
  316.5 6.3 %collective-permute-start.3 = (f32[20,8,1]{2,1,0:T(8,128)S(1)}, f32[20,8,1]{2,1,0:T(8,128)S(1)}, u32[]{:S(2)}, u32[]{:S(2)}) collective-permute-start(f32[20,8,1]{2,1,0:T(8,128)S(1)} %get-tuple-element.12), channel_id=1, source_target_pairs={{1,0},{2,1},{3,2},{4,3},{5,4},{6,5},{7,6},{8,7},{9,8},{10,9},{11,1... | collective-permute-start | bytes 1928 | tf_op jit(solution)/shard_map/ppermute | solution.py:24
  322.9 1.9 collective-permute-start.2
  325.3 49.9 %all_gather.17 = bf16[1536,320]{1,0:T(8,128)(2,1)S(1)} all-gather(bf16[96,320]{1,0:T(8,128)(2,1)S(1)} %copy-done.23), channel_id=1, replica_groups=mesh['dp'=2,'fsdp'=16,'tile'=16] {'fsdp'}, dimensions={0}, use_global_device_ids=true | all-gather | bytes 1044480 | tf_op jit(solution)/shard_map/all_gather | solution.py:144
  380.3 1.9 copy.24
  382.2 2.4 fusion.58
  384.6 2.4 reshape.187
  387.0 3.1 copy.20
  390.0 3.2 copy.21
  393.3 3.0 multiply_reduce_fusion
  400.2 1.9 concatenate.19
  402.1 3.6 convolution_bitcast_fusion
  405.7 3.0 copy.26
  408.7 2.7 concatenate.20
  415.2 7.0 %collective-permute-start.5 = (f32[8,8,1536]{2,1,0:T(8,128)}, f32[8,8,1536]{2,1,0:T(8,128)}, u32[]{:S(2)}, u32[]{:S(2)}) collective-permute-start(f32[8,8,1536]{2,1,0:T(8,128)} %get-tuple-element.6), channel_id=1, source_target_pairs={{0,15},{1,0},{2,1},{3,2},{4,3},{5,4},{6,5},{7,6},{8,7},{9,8},{10,9... | collective-permute-start | bytes 1179656 | tf_op jit(solution)/shard_map/ppermute | solution.py:32
  422.2 2.1 collective-permute-start.4
  427.0 4.3 collective-permute-done.5
  431.3 7.6 %collective-permute-done.4 = f32[8,8,1536]{2,1,0:T(8,128)} collective-permute-done((f32[8,8,1536]{2,1,0:T(8,128)}, f32[8,8,1536]{2,1,0:T(8,128)}, u32[]{:S(2)}, u32[]{:S(2)}) %collective-permute-start.4) | collective-permute-done | bytes 393248 | tf_op jit(solution)/shard_map/ppermute | solution.py:32
  438.9 1.7 fusion.6
  440.7 5.2 fusion.52
  447.4 78.6 %all-gather.9.cloned.1.call-done = f32[3072,320]{1,0:T(8,128)} async-done(((f32[96,320]{1,0:T(8,128)}), f32[3072,320]{1,0:T(8,128)}) %all-gather.9.cloned.1.call-update) | async-done | bytes 3932176 | tf_op jit(solution)/shard_map/all_gather | solution.py:179
  525.9 3.3 reduce_sum.69
  (110 shorter events, 27.9 us)
Async XLA Ops:
  7.2 3.4 copy-start.24
  7.2 96.3 %all-gather.5.cloned.1.call-start = ((), (), s32[]{:S(2)}) async-start(), calls=%async_computation.1 | async-start | bytes 7520256 | tf_op jit(solution)/shard_map/all_gather | solution.py:132
  7.9 193.3 %all-gather.7.cloned.1.call-start = ((), (), s32[]{:S(2)}) async-start(), calls=%async_computation.2 | async-start | bytes 2506752 | tf_op jit(solution)/shard_map/all_gather | solution.py:141
  8.7 307.7 %reduce-scatter.2.cloned.1.call-start = ((), (), s32[]{:S(2)}) async-start(), calls=%async_computation.3 | async-start | bytes 2506752 | tf_op jit(solution)/shard_map/reduce_scatter | solution.py:178
  108.5 9.5 %copy-start.12 = (bf16[256,2304]{1,0:T(8,128)(2,1)}, bf16[256,2304]{1,0:T(8,128)(2,1)S(1)}, u32[]{:S(2)}) copy-start(bf16[256,2304]{1,0:T(8,128)(2,1)S(1)} %convolution_convert_fusion) | copy-start | bytes 3538948
  108.5 9.5 %copy-start.22 = (f32[1,20,32,128]{3,2,1,0:T(8,128)S(1)}, f32[1,20,32,128]{3,2,1,0:T(8,128)}, u32[]{:S(2)}) copy-start(f32[1,20,32,128]{3,2,1,0:T(8,128)} %param.13) | copy-start | bytes 983044
  109.4 11.9 %collective-permute-start.1 = (bf16[8,8,1536]{2,1,0:T(8,128)(2,1)}, bf16[8,8,1536]{2,1,0:T(8,128)(2,1)}, u32[]{:S(2)}, u32[]{:S(2)}) collective-permute-start(bf16[8,8,1536]{2,1,0:T(8,128)(2,1)} %get-tuple-element.10), channel_id=1, source_target_pairs={{1,0},{2,1},{3,2},{4,3},{5,4},{6,5},{7,6},{8,7},{9,8},{10,9},{11,1... | collective-permute-start | bytes 589832 | tf_op jit(solution)/shard_map/ppermute | solution.py:24
  116.1 11.2 %collective-permute-start = (bf16[8,8,1536]{2,1,0:T(8,128)(2,1)}, bf16[8,8,1536]{2,1,0:T(8,128)(2,1)}, u32[]{:S(2)}, u32[]{:S(2)}) collective-permute-start(bf16[8,8,1536]{2,1,0:T(8,128)(2,1)} %get-tuple-element.9), channel_id=1, source_target_pairs={{0,1},{1,2},{2,3},{3,4},{4,5},{5,6},{6,7},{7,8},{8,9},{9,10},{10,1... | collective-permute-start | bytes 589832 | tf_op jit(solution)/shard_map/ppermute | solution.py:23
  120.5 83.2 %copy-start.13 = (bf16[256,320]{0,1:T(8,128)(2,1)}, bf16[256,320]{0,1:T(8,128)(2,1)S(1)}, u32[]{:S(2)}) copy-start(bf16[256,320]{0,1:T(8,128)(2,1)S(1)} %convert_element_type.125) | copy-start | bytes 491524
  121.2 7.9 %copy-start.10 = (bf16[256,768]{0,1:T(8,128)(2,1)}, bf16[256,768]{0,1:T(8,128)(2,1)S(1)}, u32[]{:S(2)}) copy-start(bf16[256,768]{0,1:T(8,128)(2,1)S(1)} %copy.18) | copy-start | bytes 1179652
  128.8 3.2 copy-start.18
  206.7 109.8 %copy-start.16 = (f32[1,20,8,32]{3,2,1,0:T(8,128)S(1)}, f32[1,20,8,32]{3,2,1,0:T(8,128)}, u32[]{:S(2)}) copy-start(f32[1,20,8,32]{3,2,1,0:T(8,128)} %param.12) | copy-start | bytes 61444
  206.7 118.7 %copy-start.23 = (bf16[96,320]{1,0:T(8,128)(2,1)S(1)}, bf16[96,320]{1,0:T(8,128)(2,1)}, u32[]{:S(2)}) copy-start(bf16[96,320]{1,0:T(8,128)(2,1)} %param.11) | copy-start | bytes 184324
  206.7 319.3 %all-gather.9.cloned.1.call-start = ((), (), s32[]{:S(2)}) async-start(), calls=%async_computation.4 | async-start | bytes 4866048 | tf_op jit(solution)/shard_map/all_gather | solution.py:179
  316.5 61.0 %collective-permute-start.3 = (f32[20,8,1]{2,1,0:T(8,128)S(1)}, f32[20,8,1]{2,1,0:T(8,128)S(1)}, u32[]{:S(2)}, u32[]{:S(2)}) collective-permute-start(f32[20,8,1]{2,1,0:T(8,128)S(1)} %get-tuple-element.12), channel_id=1, source_target_pairs={{1,0},{2,1},{3,2},{4,3},{5,4},{6,5},{7,6},{8,7},{9,8},{10,9},{11,1... | collective-permute-start | bytes 1928 | tf_op jit(solution)/shard_map/ppermute | solution.py:24
  322.9 54.6 %collective-permute-start.2 = (f32[20,8,1]{2,1,0:T(8,128)S(1)}, f32[20,8,1]{2,1,0:T(8,128)S(1)}, u32[]{:S(2)}, u32[]{:S(2)}) collective-permute-start(f32[20,8,1]{2,1,0:T(8,128)S(1)} %get-tuple-element.11), channel_id=1, source_target_pairs={{0,1},{1,2},{2,3},{3,4},{4,5},{5,6},{6,7},{7,8},{8,9},{9,10},{10,1... | collective-permute-start | bytes 1928 | tf_op jit(solution)/shard_map/ppermute | solution.py:23
  375.3 3.5 copy-start.4
  390.0 3.2 copy-start.19
  390.0 3.2 copy-start.20
  393.3 3.0 copy-start.3
  412.7 11.6 %copy-start.2 = (bf16[8,256,384]{2,1,0:T(8,128)(2,1)S(1)}, bf16[8,256,384]{2,1,0:T(8,128)(2,1)}, u32[]{:S(2)}) copy-start(bf16[8,256,384]{2,1,0:T(8,128)(2,1)} %copy-done.1) | copy-start | bytes 4718596
  412.7 11.6 %copy-start.8 = (bf16[384,768]{0,1:T(8,128)(2,1)S(1)}, bf16[384,768]{0,1:T(8,128)(2,1)}, u32[]{:S(2)}) copy-start(bf16[384,768]{0,1:T(8,128)(2,1)} %copy-done.7) | copy-start | bytes 1769476
  415.2 16.1 %collective-permute-start.5 = (f32[8,8,1536]{2,1,0:T(8,128)}, f32[8,8,1536]{2,1,0:T(8,128)}, u32[]{:S(2)}, u32[]{:S(2)}) collective-permute-start(f32[8,8,1536]{2,1,0:T(8,128)} %get-tuple-element.6), channel_id=1, source_target_pairs={{0,15},{1,0},{2,1},{3,2},{4,3},{5,4},{6,5},{7,6},{8,7},{9,8},{10,9... | collective-permute-start | bytes 1179656 | tf_op jit(solution)/shard_map/ppermute | solution.py:32
  422.2 3.7 copy-start.14
  422.2 3.7 copy-start.15
  422.2 3.7 copy-start.26
  422.2 3.7 copy-start.27
  422.2 3.7 copy-start.28
  422.2 3.7 copy-start.29
  422.2 16.7 %collective-permute-start.4 = (f32[8,8,1536]{2,1,0:T(8,128)}, f32[8,8,1536]{2,1,0:T(8,128)}, u32[]{:S(2)}, u32[]{:S(2)}) collective-permute-start(f32[8,8,1536]{2,1,0:T(8,128)} %get-tuple-element.5), channel_id=1, source_target_pairs={{0,1},{1,2},{2,3},{3,4},{4,5},{5,6},{6,7},{7,8},{8,9},{9,10},{10,1... | collective-permute-start | bytes 1179656 | tf_op jit(solution)/shard_map/ppermute | solution.py:32
  427.0 13.6 %copy-start.21 = (bf16[256,768]{1,0:T(8,128)(2,1)S(1)}, bf16[256,768]{1,0:T(8,128)(2,1)}, u32[]{:S(2)}) copy-start(bf16[256,768]{1,0:T(8,128)(2,1)} %copy.27) | copy-start | bytes 1179652
  427.0 13.6 %copy-start.25 = (f32[1536]{0:T(1024)S(1)}, f32[1536]{0:T(1024)}, u32[]{:S(2)}) copy-start(f32[1536]{0:T(1024)} %param.8) | copy-start | bytes 18436
  (9 other events, 15.7 us)
Sparse Core Ops, SparseCore 0:
  10.1 93.3 all-gather.4
  105.6 95.5 all-gather.6
  206.8 109.5 reduce-scatter.1
  320.5 205.3 all-gather.8
